TPU v7x, 32 devices: a whole 2x2x4 slice. The times are simulated.
32 devices in a mesh: ctx: 8 (over z, y), head: 4 (over x, core).
Axes of the slice: x: 2, y: 2, z: 4, core: 2. Of those that a mesh axis runs over, the one named last changes fastest.
Arguments:
- queries: bfloat16 [1024, 64, 128], P('ctx', 'head'), may hold values from -90 to 90
- key_states: bfloat16 [1024, 8, 128], P('ctx', 'head'), may hold values from -4.5 to 4.5
- value_states: bfloat16 [1024, 8, 128], P('ctx', 'head'), may hold values from -6 to 6
- chosen: int32 [2, 4], replicated, may hold values from 0 to 1, as said below
- valid_count: int32 [2], replicated, may hold values from 1 to 2, as said below
Outputs:
- attn_out: bfloat16 [1024, 64, 128], P('ctx', 'head')
- key_mass: float32 [64, 1024], P('head', 'ctx')
Inputs may be any that keep to these rules, and one draw needn't show every extreme that they name: `chosen`: row i lists block i first; if valid_count[i] >= 2, block 0 second; the next valid_count[i] - 2 entries are distinct blocks from 1 to i - 1; entries from position valid_count[i] on equal i. valid_count[i] is at most min(4, i + 1), and the last block's count is min(4, 2).
All inputs are finite; a program needn't handle non-finite values.
Results may differ from a plain program's by a relative error of at most 0.0046.
Values may be sent and summed in bfloat16 or wider, within the bound.
A program may use at most 64 MiB of HBM per device.

v0:
```python
import math
import jax
import jax.numpy as jnp
from jax import lax
from jax.sharding import PartitionSpec as P

BLOCK = 512


def from_partner(value, axis, bit):
    mask = 2**bit
    pairs = [(source, source ^ mask) for source in range(lax.axis_size(axis))]
    return lax.ppermute(value, axis, pairs)


def on_device(queries, key_states, value_states, chosen, valid_count):
    ctx_size = lax.axis_size("ctx")
    my_index = lax.axis_index("ctx")
    token_count = queries.shape[0]
    query_heads = queries.shape[1]
    head_depth = queries.shape[2]
    kv_total = key_states.shape[1]
    groups = query_heads // kv_total
    slot_total = chosen.shape[1]
    split_count = BLOCK // token_count
    quarter = token_count // split_count
    my_block = my_index // split_count
    my_member = my_index % split_count
    listed = chosen[my_block]
    slot_ids = jnp.arange(slot_total)
    slot_valid = slot_ids < valid_count[my_block]
    owners = jnp.arange(ctx_size) // split_count
    wanted = jnp.any(
        (slot_ids[None, :] < valid_count[owners][:, None]) & (chosen[owners] == my_block), axis=1
    )
    stacked = jnp.stack([key_states, value_states]).reshape(
        2, 1, split_count, quarter, kv_total, head_depth
    )
    outgoing = jnp.broadcast_to(
        stacked, (2, ctx_size // split_count, split_count, quarter, kv_total, head_depth)
    )
    outgoing = outgoing.reshape(2, ctx_size, quarter, kv_total, head_depth)
    outgoing = jnp.where(wanted[None, :, None, None, None], outgoing, jnp.zeros((), outgoing.dtype))
    incoming = lax.all_to_all(outgoing, "ctx", split_axis=1, concat_axis=1, tiled=True)
    sources = (listed[:, None] * split_count + jnp.arange(split_count)[None, :]).reshape(-1)
    fetched = jnp.take(incoming, sources, axis=1)
    bit_total = split_count.bit_length() - 1
    for bit_index in range(bit_total):
        partner = from_partner(fetched, "ctx", bit_index)
        is_lower = my_member // 2**bit_index % 2 == 0
        fetched = jnp.where(
            is_lower,
            jnp.concatenate([fetched, partner], axis=2),
            jnp.concatenate([partner, fetched], axis=2),
        )
    fetched = fetched.reshape(2, slot_total * BLOCK, kv_total, head_depth)
    by_head = jnp.transpose(fetched, (0, 2, 1, 3))
    query_pos = my_index * token_count + jnp.arange(token_count)
    score_scale = 1.0 / math.sqrt(head_depth)
    grouped = queries.reshape(token_count, kv_total, groups, head_depth)
    offsets = jnp.arange(BLOCK)
    key_pos = (listed[:, None] * BLOCK + offsets[None, :]).reshape(-1)
    key_block = jnp.repeat(listed, BLOCK)
    key_valid = jnp.repeat(slot_valid, BLOCK)
    visibility = key_valid[None, :] & (
        (key_block[None, :] < my_block) | (key_pos[None, :] <= query_pos[:, None])
    )
    contract_last = (((1,), (1,)), ((), ()))
    head_outputs = []
    head_masses = []
    for kv_head in range(kv_total):
        key_head = by_head[0, kv_head]
        value_head = by_head[1, kv_head]
        for group_index in range(groups):
            raw_scores = (
                lax.dot_general(
                    grouped[:, kv_head, group_index],
                    key_head,
                    contract_last,
                    preferred_element_type=jnp.float32,
                )
                * score_scale
            )
            scores = jnp.where(visibility, raw_scores, -jnp.inf)
            highest = jnp.max(scores, axis=-1, keepdims=True)
            raised = jnp.exp(scores - highest)
            attention = raised / jnp.sum(raised, axis=-1, keepdims=True)
            head_outputs.append(
                jnp.dot(
                    attention.astype(jnp.bfloat16), value_head, preferred_element_type=jnp.float32
                )
            )
            head_masses.append(jnp.sum(attention, axis=0).reshape(slot_total, BLOCK))
    attn_out = jnp.stack(head_outputs, axis=1).astype(jnp.bfloat16)
    contrib = jnp.stack(head_masses, axis=1).reshape(
        slot_total, query_heads, split_count, token_count
    )
    contrib = jnp.transpose(contrib, (0, 2, 1, 3)).reshape(
        slot_total * split_count, query_heads, token_count
    )
    landing = jnp.zeros((ctx_size, query_heads, token_count), jnp.float32).at[sources].add(contrib)
    key_mass = lax.psum_scatter(landing, "ctx", scatter_dimension=0, tiled=True).reshape(
        query_heads, token_count
    )
    return (attn_out, key_mass)


def solution(mesh):
    in_specs = (P("ctx", "head", None), P("ctx", "head", None), P("ctx", "head", None), P(), P())
    out_specs = (P("ctx", "head", None), P("head", "ctx"))
    return jax.shard_map(
        on_device, mesh=mesh, in_specs=in_specs, out_specs=out_specs, check_vma=False
    )
```

profile of v0, /device:TPU:0, one launch (start us, length us, event | category | flops | bytes accessed | tf_op | source)
XLA Modules:
  0.0 163.1 jit_solution(17696914821971063014)
XLA Ops:
  7.2 1.2 gather_fusion.1
  8.5 1.3 gather_fusion
  9.8 1.1 maximum_bitcast_fusion
  11.9 7.3 %all-to-all-start = ((bf16[2,8,32,2,128]{4,2,3,0,1:T(8,128)(2,1)}), bf16[2,8,32,2,128]{4,2,3,0,1:T(8,128)(2,1)S(1)}, u32[]{:S(2)}, u32[]{:S(2)}) async-start(bf16[2,8,32,2,128]{4,2,3,0,1:T(8,128)(2,1)} %bitcast_select_fusion), calls=%async_computation | async-start | bytes 524288 | tf_op jit(solution)/shard_map/all_to_all | solution.py:44
  20.1 7.9 %all-to-all-done = bf16[2,8,32,2,128]{4,2,3,0,1:T(8,128)(2,1)S(1)} async-done(((bf16[2,8,32,2,128]{4,2,3,0,1:T(8,128)(2,1)}), bf16[2,8,32,2,128]{4,2,3,0,1:T(8,128)(2,1)S(1)}, u32[]{:S(2)}, u32[]{:S(2)}) %all-to-all-start) | async-done | bytes 262176 | tf_op jit(solution)/shard_map/all_to_all | solution.py:44
  28.9 1.5 collective-permute-start
  30.4 10.4 %collective-permute-done = bf16[2,16,32,2,128]{4,2,3,0,1:T(8,128)(2,1)S(1)} collective-permute-done((bf16[2,16,32,2,128]{4,2,3,0,1:T(8,128)(2,1)S(1)}, bf16[2,16,32,2,128]{4,2,3,0,1:T(8,128)(2,1)S(1)}, u32[]{:S(2)}, u32[]{:S(2)}) %collective-permute-start) | collective-permute-done | bytes 524320 | tf_op jit(solution)/shard_map/ppermute | solution.py:13
  43.4 1.2 copy.18
  44.6 18.8 %collective-permute-done.1 = bf16[2,16,64,2,128]{4,2,3,0,1:T(8,128)(2,1)S(1)} collective-permute-done((bf16[2,16,64,2,128]{4,2,3,0,1:T(8,128)(2,1)S(1)}, bf16[2,16,64,2,128]{4,2,3,0,1:T(8,128)(2,1)S(1)}, u32[]{:S(2)}, u32[]{:S(2)}) %collective-permute-start.1) | collective-permute-done | bytes 1048608 | tf_op jit(solution)/shard_map/ppermute | solution.py:13
  65.3 0.9 fusion.163
  66.2 0.9 fusion.162
  67.1 0.9 fusion.161
  73.5 1.1 fusion.154
  79.8 1.0 fusion.33
  91.1 1.1 scatter_fusion
  92.9 2.5 %fusion.35 = bf16[128,16,128]{2,0,1:T(8,128)(2,1)} fusion(bf16[128,16,128]{2,0,1:T(8,128)(2,1)} %fusion.33, f32[128,2048]{0,1:T(8,128)} %copy-done.23, f32[128]{0:T(128)S(1)} %fusion.67, f32[128]{0:T(128)S(1)} %get-tuple-element.18, bf16[2,2,2048,128]{3,2,1,0:T(8,128)(2,1)} %bitcast.347), kind=kOutput, calls=%fused_computation.72 | convolution fusion | flops 67911680 | bytes 1606656 | tf_op jit(solution)/shard_map/dot_general | solution.py:89
  95.4 1.0 fusion.37
  96.6 1.0 fusion.39
  97.9 1.0 fusion.41
  99.1 1.0 fusion.43
  100.3 1.0 fusion.45
  101.5 1.0 fusion.47
  102.8 1.0 fusion.49
  104.0 1.0 fusion.51
  105.2 1.0 fusion.53
  106.5 1.0 fusion.55
  107.7 1.0 fusion.57
  108.6 1.0 fusion.59
  109.6 1.0 fusion.61
  110.6 1.0 fusion.63
  111.5 2.2 %copy.19 = bf16[128,16,128]{2,1,0:T(8,128)(2,1)} copy(bf16[128,16,128]{2,0,1:T(8,128)(2,1)} %fusion.63) | data formatting | bytes 1048576
  113.7 42.6 %reduce-scatter.2.cloned.1.call-done = f32[1,16,128]{2,1,0:T(8,128)} async-done(((f32[8,16,128]{2,1,0:T(8,128)}), f32[1,16,128]{2,1,0:T(8,128)}) %reduce-scatter.2.cloned.1.call-update) | async-done | bytes 8208 | tf_op jit(solution)/shard_map/reduce_scatter | solution.py:102
  (135 shorter events, 31.3 us)
Async XLA Ops:
  11.9 16.2 %all-to-all-start = ((bf16[2,8,32,2,128]{4,2,3,0,1:T(8,128)(2,1)}), bf16[2,8,32,2,128]{4,2,3,0,1:T(8,128)(2,1)S(1)}, u32[]{:S(2)}, u32[]{:S(2)}) async-start(bf16[2,8,32,2,128]{4,2,3,0,1:T(8,128)(2,1)} %bitcast_select_fusion), calls=%async_computation | async-start | bytes 524288 | tf_op jit(solution)/shard_map/all_to_all | solution.py:44
  19.1 137.2 %reduce-scatter.2.cloned.1.call-start = ((), (), s32[]{:S(2)}) async-start(), calls=%async_computation.2 | async-start | bytes 73728 | tf_op jit(solution)/shard_map/reduce_scatter | solution.py:102
  28.1 13.8 %copy-start = (s32[2]{0:T(128)S(1)}, s32[2]{0:T(128)}, u32[]{:S(2)}) copy-start(s32[2]{0:T(128)} %param.9) | copy-start | bytes 28
  28.1 14.4 %copy-start.26 = (s32[2,4]{1,0:T(2,128)S(1)}, s32[2,4]{1,0:T(2,128)}, u32[]{:S(2)}) copy-start(s32[2,4]{1,0:T(2,128)} %param.8) | copy-start | bytes 100
  28.9 11.9 %collective-permute-start = (bf16[2,16,32,2,128]{4,2,3,0,1:T(8,128)(2,1)S(1)}, bf16[2,16,32,2,128]{4,2,3,0,1:T(8,128)(2,1)S(1)}, u32[]{:S(2)}, u32[]{:S(2)}) collective-permute-start(bf16[2,16,32,2,128]{4,2,3,0,1:T(8,128)(2,1)S(1)} %select_bitcast_fusion), channel_id=1, source_target_pairs={{0,4},{4,0},{8,12},{12,8},{16,20},{20,16},{24,28},{28,24},{1,5},{5... | collective-permute-start | bytes 1572872 | tf_op jit(solution)/shard_map/ppermute | solution.py:13
  41.1 22.2 %collective-permute-start.1 = (bf16[2,16,64,2,128]{4,2,3,0,1:T(8,128)(2,1)S(1)}, bf16[2,16,64,2,128]{4,2,3,0,1:T(8,128)(2,1)S(1)}, u32[]{:S(2)}, u32[]{:S(2)}) collective-permute-start(bf16[2,16,64,2,128]{4,2,3,0,1:T(8,128)(2,1)S(1)} %maximum_select_fusion.1), channel_id=1, source_target_pairs={{0,8},{4,12},{8,0},{12,4},{16,24},{20,28},{24,16},{28,20},{1,9},{5... | collective-permute-start | bytes 3145736 | tf_op jit(solution)/shard_map/ppermute | solution.py:13
  64.4 15.4 %copy-start.24 = (bf16[2,16,128,2,128]{4,2,1,3,0:T(8,128)(2,1)}, bf16[2,16,128,2,128]{4,2,1,3,0:T(8,128)(2,1)S(1)}, u32[]{:S(2)}) copy-start(bf16[2,16,128,2,128]{4,2,1,3,0:T(8,128)(2,1)S(1)} %copy.17) | copy-start | bytes 6291460
  68.0 15.0 %copy-start.1 = (f32[128,2048]{0,1:T(8,128)}, f32[128,2048]{0,1:T(8,128)S(1)}, u32[]{:S(2)}) copy-start(f32[128,2048]{0,1:T(8,128)S(1)} %get-tuple-element.41) | copy-start | bytes 3145732
  68.9 14.8 %copy-start.3 = (f32[128,2048]{0,1:T(8,128)}, f32[128,2048]{0,1:T(8,128)S(1)}, u32[]{:S(2)}) copy-start(f32[128,2048]{0,1:T(8,128)S(1)} %get-tuple-element.39) | copy-start | bytes 3145732
  69.8 14.5 %copy-start.5 = (f32[128,2048]{0,1:T(8,128)}, f32[128,2048]{0,1:T(8,128)S(1)}, u32[]{:S(2)}) copy-start(f32[128,2048]{0,1:T(8,128)S(1)} %get-tuple-element.37) | copy-start | bytes 3145732
  70.8 14.3 %copy-start.7 = (f32[128,2048]{0,1:T(8,128)}, f32[128,2048]{0,1:T(8,128)S(1)}, u32[]{:S(2)}) copy-start(f32[128,2048]{0,1:T(8,128)S(1)} %get-tuple-element.35) | copy-start | bytes 3145732
  71.7 14.0 %copy-start.9 = (f32[128,2048]{0,1:T(8,128)}, f32[128,2048]{0,1:T(8,128)S(1)}, u32[]{:S(2)}) copy-start(f32[128,2048]{0,1:T(8,128)S(1)} %get-tuple-element.33) | copy-start | bytes 3145732
  72.6 13.8 %copy-start.11 = (f32[128,2048]{0,1:T(8,128)}, f32[128,2048]{0,1:T(8,128)S(1)}, u32[]{:S(2)}) copy-start(f32[128,2048]{0,1:T(8,128)S(1)} %get-tuple-element.31) | copy-start | bytes 3145732
  73.5 13.5 %copy-start.13 = (f32[128,2048]{0,1:T(8,128)}, f32[128,2048]{0,1:T(8,128)S(1)}, u32[]{:S(2)}) copy-start(f32[128,2048]{0,1:T(8,128)S(1)} %get-tuple-element.29) | copy-start | bytes 3145732
  74.6 13.3 %copy-start.15 = (f32[128,2048]{0,1:T(8,128)}, f32[128,2048]{0,1:T(8,128)S(1)}, u32[]{:S(2)}) copy-start(f32[128,2048]{0,1:T(8,128)S(1)} %get-tuple-element.27) | copy-start | bytes 3145732
  75.5 13.0 %copy-start.17 = (f32[128,2048]{0,1:T(8,128)}, f32[128,2048]{0,1:T(8,128)S(1)}, u32[]{:S(2)}) copy-start(f32[128,2048]{0,1:T(8,128)S(1)} %get-tuple-element.25) | copy-start | bytes 3145732
  76.4 12.8 %copy-start.19 = (f32[128,2048]{0,1:T(8,128)}, f32[128,2048]{0,1:T(8,128)S(1)}, u32[]{:S(2)}) copy-start(f32[128,2048]{0,1:T(8,128)S(1)} %get-tuple-element.23) | copy-start | bytes 3145732
  77.3 12.5 %copy-start.21 = (f32[128,2048]{0,1:T(8,128)}, f32[128,2048]{0,1:T(8,128)S(1)}, u32[]{:S(2)}) copy-start(f32[128,2048]{0,1:T(8,128)S(1)} %get-tuple-element.21) | copy-start | bytes 3145732
  78.2 12.3 %copy-start.23 = (f32[128,2048]{0,1:T(8,128)}, f32[128,2048]{0,1:T(8,128)S(1)}, u32[]{:S(2)}) copy-start(f32[128,2048]{0,1:T(8,128)S(1)} %get-tuple-element.19) | copy-start | bytes 3145732
  92.3 0.6 copy-start.27
  92.9 2.5 %copy-start.22 = (f32[128,2048]{0,1:T(8,128)S(1)}, f32[128,2048]{0,1:T(8,128)}, u32[]{:S(2)}) copy-start(f32[128,2048]{0,1:T(8,128)} %copy-done.21) | copy-start | bytes 3145732
  92.9 2.5 %copy-start.25 = (bf16[2,16,128,2,128]{4,2,1,3,0:T(8,128)(2,1)S(1)}, bf16[2,16,128,2,128]{4,2,1,3,0:T(8,128)(2,1)}, u32[]{:S(2)}) copy-start(bf16[2,16,128,2,128]{4,2,1,3,0:T(8,128)(2,1)} %copy-done.24) | copy-start | bytes 6291460
  95.4 1.2 copy-start.20
  96.6 1.2 copy-start.18
  97.9 1.2 copy-start.16
  99.1 1.2 copy-start.14
  100.3 1.2 copy-start.12
  101.5 1.2 copy-start.10
  102.8 1.2 copy-start.8
  104.0 1.2 copy-start.6
  105.2 1.2 copy-start.4
  106.5 1.2 copy-start.2
Sparse Core Ops, SparseCore 0:
  93.0 63.2 reduce-scatter.1
where the time goes:
time: 164 us; the launch traced here: 163 us
  waiting for transfers between devices  79.7 us (49%)
  matrix products  31.6 us (19%)
  other arithmetic  16.6 us (10%)
  between operations  14.5 us (9%)
  local copies, waits for them, and re-layouts  11.3 us (7%)
  starting transfers between devices  9.52 us (6%)
    reduce_scatter x1, waiting for transfers between devices, on_device(): lax.psum_scatter(landing, 'ctx', scatter_dimension=0, tiled=True)  42.6 us
    ppermute x2, waiting for transfers between devices, from_partner(): return lax.ppermute(value, axis, pairs)  29.2 us
    dot_general x16, matrix products, on_device(): jnp.dot(attention.astype(jnp.bfloat16), value_head, preferred_element_typ...  16.9 us
    dot_general x16, matrix products, on_device(): lax.dot_general(grouped[:, kv_head, group_index], key_head, contract_last...  14.7 us
    all_to_all x1, waiting for transfers between devices, on_device(): lax.all_to_all(outgoing, 'ctx', split_axis=1, concat_axis=1, tiled=True)  7.9 us
    all_to_all x1, starting transfers between devices, on_device(): lax.all_to_all(outgoing, 'ctx', split_axis=1, concat_axis=1, tiled=True)  7.28 us
    unnamed x63, local copies, waits for them, and re-layouts  6.8 us
    reduce_sum x16, other arithmetic, on_device(): head_masses.append(jnp.sum(attention, axis=0).reshape(slot_total, BLOCK))  5.65 us
  transfers between devices with their start and end apart: 4, of which 4 were waited for; matrix products, arithmetic and copies ran while one was open for 13% of the time, Pallas kernels for 0%

commit v1 on v0

--- a/solution.py
+++ b/solution.py
@@ -41,7 +41,19 @@
     )
     outgoing = outgoing.reshape(2, ctx_size, quarter, kv_total, head_depth)
     outgoing = jnp.where(wanted[None, :, None, None, None], outgoing, jnp.zeros((), outgoing.dtype))
-    incoming = lax.all_to_all(outgoing, "ctx", split_axis=1, concat_axis=1, tiled=True)
+    ways, here = (lax.axis_size("ctx"), lax.axis_index("ctx"))
+    width = outgoing.shape[1] // ways
+    shape = list(outgoing.shape)
+    shape[1] = width
+    height = shape[1]
+    shape[1] = height * ways
+    full = jnp.zeros(shape, outgoing.dtype)
+    for mask_2 in range(ways):
+        part = lax.dynamic_slice_in_dim(outgoing, (here ^ mask_2) * width, width, axis=1)
+        if mask_2:
+            part = lax.ppermute(part, "ctx", [(d, d ^ mask_2) for d in range(ways)])
+        full = lax.dynamic_update_slice_in_dim(full, part, (here ^ mask_2) * height, axis=1)
+    incoming = full
     sources = (listed[:, None] * split_count + jnp.arange(split_count)[None, :]).reshape(-1)
     fetched = jnp.take(incoming, sources, axis=1)
     bit_total = split_count.bit_length() - 1

time: 164 us -> 160 us (0.976)
  waiting for transfers between devices: 79.7 us -> 74.4 us
  starting transfers between devices: 9.52 us -> 13.3 us
    ppermute x0 -> x7, starting transfers between devices: none -> 12.6 us  [on_device(): part = lax.ppermute(part, 'ctx', [(d, d ^ mask_2) for d in range(ways)])]
    all_to_all x1 -> x0, waiting for transfers between devices: 7.9 us -> none  [on_device(): lax.all_to_all(outgoing, 'ctx', split_axis=1, concat_axis=1, tiled=True)]
    all_to_all x1 -> x0, starting transfers between devices: 7.28 us -> none  [on_device(): lax.all_to_all(outgoing, 'ctx', split_axis=1, concat_axis=1, tiled=True)]
    ppermute x0 -> x7, waiting for transfers between devices: none -> 6.51 us  [on_device(): part = lax.ppermute(part, 'ctx', [(d, d ^ mask_2) for d in range(ways)])]
    reduce_scatter x1, waiting for transfers between devices: 42.6 us -> 38.1 us  [on_device(): lax.psum_scatter(landing, 'ctx', scatter_dimension=0, tiled=True)]
    unnamed x63 -> x65, local copies, waits for them, and re-layouts: 6.8 us -> 5.79 us
  transfers between devices with their start and end apart: 4 -> 10, of which waited for: 4 -> 6; matrix products, arithmetic and copies ran while one was open for 13% -> 13% of each run, Pallas kernels for 0% -> 0%
where the time goes in v1:
time: 160 us
  waiting for transfers between devices  74.4 us (47%)
  matrix products  31.6 us (20%)
  other arithmetic  15.2 us (10%)
  between operations  14.7 us (9%)
  starting transfers between devices  13.3 us (8%)
  local copies, waits for them, and re-layouts  10.4 us (6%)
    reduce_scatter x1, waiting for transfers between devices, on_device(): lax.psum_scatter(landing, 'ctx', scatter_dimension=0, tiled=True)  38.1 us
    ppermute x2, waiting for transfers between devices, from_partner(): return lax.ppermute(value, axis, pairs)  29.8 us
    dot_general x16, matrix products, on_device(): jnp.dot(attention.astype(jnp.bfloat16), value_head, preferred_element_typ...  16.9 us
    dot_general x16, matrix products, on_device(): lax.dot_general(grouped[:, kv_head, group_index], key_head, contract_last...  14.7 us
    ppermute x7, starting transfers between devices, on_device(): part = lax.ppermute(part, 'ctx', [(d, d ^ mask_2) for d in range(ways)])  12.6 us
    ppermute x7, waiting for transfers between devices, on_device(): part = lax.ppermute(part, 'ctx', [(d, d ^ mask_2) for d in range(ways)])  6.51 us
    unnamed x65, local copies, waits for them, and re-layouts  5.79 us
    reduce_sum x16, other arithmetic, on_device(): head_masses.append(jnp.sum(attention, axis=0).reshape(slot_total, BLOCK))  5.65 us
  transfers between devices with their start and end apart: 10, of which 6 were waited for; matrix products, arithmetic and copies ran while one was open for 13% of the time, Pallas kernels for 0%

profile of v1, /device:TPU:0, one launch (start us, length us, event | category | flops | bytes accessed | tf_op | source)
XLA Modules:
  0.0 159.7 jit_solution(13690630826689850009)
XLA Ops:
  7.3 1.2 gather_fusion.1
  8.5 1.3 gather_fusion
  9.8 1.1 maximum_bitcast_fusion
  11.4 3.0 %collective-permute-start = (bf16[2,1,32,2,128]{4,2,3,1,0:T(8,128)(2,1)S(1)}, bf16[2,1,32,2,128]{4,2,3,1,0:T(8,128)(2,1)S(1)}, u32[]{:S(2)}, u32[]{:S(2)}) collective-permute-start(bf16[2,1,32,2,128]{4,2,3,1,0:T(8,128)(2,1)S(1)} %get-tuple-element.14), channel_id=1, source_target_pairs={{0,4},{4,0},{8,12},{12,8},{16,20},{20,16},{24,28},{28,24},{1,5},{5... | collective-permute-start | bytes 98312 | tf_op jit(solution)/shard_map/ppermute | solution.py:54
  14.5 1.6 collective-permute-start.1
  16.0 3.0 %collective-permute-start.3 = (bf16[2,1,32,2,128]{4,2,3,1,0:T(8,128)(2,1)S(1)}, bf16[2,1,32,2,128]{4,2,3,1,0:T(8,128)(2,1)S(1)}, u32[]{:S(2)}, u32[]{:S(2)}) collective-permute-start(bf16[2,1,32,2,128]{4,2,3,1,0:T(8,128)(2,1)S(1)} %get-tuple-element.11), channel_id=1, source_target_pairs={{0,16},{4,20},{8,24},{12,28},{16,0},{20,4},{24,8},{28,12},{1,17},{... | collective-permute-start | bytes 98312 | tf_op jit(solution)/shard_map/ppermute | solution.py:54
  19.0 1.3 collective-permute-start.4
  20.6 3.7 %collective-permute-start.5 = (bf16[2,1,32,2,128]{4,2,3,1,0:T(8,128)(2,1)S(1)}, bf16[2,1,32,2,128]{4,2,3,1,0:T(8,128)(2,1)S(1)}, u32[]{:S(2)}, u32[]{:S(2)}) collective-permute-start(bf16[2,1,32,2,128]{4,2,3,1,0:T(8,128)(2,1)S(1)} %get-tuple-element.9), channel_id=1, source_target_pairs={{0,24},{4,28},{8,16},{12,20},{16,8},{20,12},{24,0},{28,4},{1,25},{... | collective-permute-start | bytes 98312 | tf_op jit(solution)/shard_map/ppermute | solution.py:54
  24.7 1.6 %collective-permute-done.5 = bf16[2,1,32,2,128]{4,2,3,1,0:T(8,128)(2,1)S(1)} collective-permute-done((bf16[2,1,32,2,128]{4,2,3,1,0:T(8,128)(2,1)S(1)}, bf16[2,1,32,2,128]{4,2,3,1,0:T(8,128)(2,1)S(1)}, u32[]{:S(2)}, u32[]{:S(2)}) %collective-permute-start.5) | collective-permute-done | bytes 32800 | tf_op jit(solution)/shard_map/ppermute | solution.py:54
  26.4 4.6 %collective-permute-done.6 = bf16[2,1,32,2,128]{4,2,3,1,0:T(8,128)(2,1)S(1)} collective-permute-done((bf16[2,1,32,2,128]{4,2,3,1,0:T(8,128)(2,1)S(1)}, bf16[2,1,32,2,128]{4,2,3,1,0:T(8,128)(2,1)S(1)}, u32[]{:S(2)}, u32[]{:S(2)}) %collective-permute-start.6) | collective-permute-done | bytes 32800 | tf_op jit(solution)/shard_map/ppermute | solution.py:54
  32.3 10.4 %collective-permute-done.7 = bf16[2,16,32,2,128]{4,2,3,0,1:T(8,128)(2,1)S(1)} collective-permute-done((bf16[2,16,32,2,128]{4,2,3,0,1:T(8,128)(2,1)S(1)}, bf16[2,16,32,2,128]{4,2,3,0,1:T(8,128)(2,1)S(1)}, u32[]{:S(2)}, u32[]{:S(2)}) %collective-permute-start.7) | collective-permute-done | bytes 524320 | tf_op jit(solution)/shard_map/ppermute | solution.py:13
  44.9 19.5 %collective-permute-done.8 = bf16[2,16,64,2,128]{4,2,3,0,1:T(8,128)(2,1)S(1)} collective-permute-done((bf16[2,16,64,2,128]{4,2,3,0,1:T(8,128)(2,1)S(1)}, bf16[2,16,64,2,128]{4,2,3,0,1:T(8,128)(2,1)S(1)}, u32[]{:S(2)}, u32[]{:S(2)}) %collective-permute-start.8) | collective-permute-done | bytes 1048608 | tf_op jit(solution)/shard_map/ppermute | solution.py:13
  73.6 1.1 fusion.155
  80.8 1.0 fusion.33
  92.1 1.1 scatter_fusion
  94.0 2.5 %fusion.35 = bf16[128,16,128]{2,0,1:T(8,128)(2,1)} fusion(bf16[128,16,128]{2,0,1:T(8,128)(2,1)} %fusion.33, f32[128,2048]{0,1:T(8,128)} %copy-done.23, f32[128]{0:T(128)S(1)} %fusion.67, f32[128]{0:T(128)S(1)} %get-tuple-element.24, bf16[2,2,2048,128]{3,2,1,0:T(8,128)(2,1)} %bitcast.346), kind=kOutput, calls=%fused_computation.72 | convolution fusion | flops 67911680 | bytes 1606656 | tf_op jit(solution)/shard_map/dot_general | solution.py:101
  96.5 1.0 fusion.37
  97.7 1.0 fusion.39
  98.9 1.0 fusion.41
  100.1 1.0 fusion.43
  101.4 1.0 fusion.45
  102.6 1.0 fusion.47
  103.8 1.0 fusion.49
  105.0 1.0 fusion.51
  106.3 1.0 fusion.53
  107.5 1.0 fusion.55
  108.7 1.0 fusion.57
  109.7 1.0 fusion.59
  110.7 1.0 fusion.61
  111.6 1.0 fusion.63
  112.6 2.2 %copy.14 = bf16[128,16,128]{2,1,0:T(8,128)(2,1)} copy(bf16[128,16,128]{2,0,1:T(8,128)(2,1)} %fusion.63) | data formatting | bytes 1048576
  114.8 38.1 %reduce-scatter.2.cloned.1.call-done = f32[1,16,128]{2,1,0:T(8,128)} async-done(((f32[8,16,128]{2,1,0:T(8,128)}), f32[1,16,128]{2,1,0:T(8,128)}) %reduce-scatter.2.cloned.1.call-update) | async-done | bytes 8208 | tf_op jit(solution)/shard_map/reduce_scatter | solution.py:114
  (158 shorter events, 33.4 us)
Async XLA Ops:
  7.2 13.2 %copy-start.26 = (s32[2,4]{1,0:T(2,128)S(1)}, s32[2,4]{1,0:T(2,128)}, u32[]{:S(2)}) copy-start(s32[2,4]{1,0:T(2,128)} %param.8) | copy-start | bytes 100
  7.2 145.7 %reduce-scatter.2.cloned.1.call-start = ((), (), s32[]{:S(2)}) async-start(), calls=%async_computation.1 | async-start | bytes 73728 | tf_op jit(solution)/shard_map/reduce_scatter | solution.py:114
  11.4 9.2 %collective-permute-start = (bf16[2,1,32,2,128]{4,2,3,1,0:T(8,128)(2,1)S(1)}, bf16[2,1,32,2,128]{4,2,3,1,0:T(8,128)(2,1)S(1)}, u32[]{:S(2)}, u32[]{:S(2)}) collective-permute-start(bf16[2,1,32,2,128]{4,2,3,1,0:T(8,128)(2,1)S(1)} %get-tuple-element.14), channel_id=1, source_target_pairs={{0,4},{4,0},{8,12},{12,8},{16,20},{20,16},{24,28},{28,24},{1,5},{5... | collective-permute-start | bytes 98312 | tf_op jit(solution)/shard_map/ppermute | solution.py:54
  14.5 9.8 %collective-permute-start.1 = (bf16[2,1,32,2,128]{4,2,3,1,0:T(8,128)(2,1)S(1)}, bf16[2,1,32,2,128]{4,2,3,1,0:T(8,128)(2,1)S(1)}, u32[]{:S(2)}, u32[]{:S(2)}) collective-permute-start(bf16[2,1,32,2,128]{4,2,3,1,0:T(8,128)(2,1)S(1)} %get-tuple-element.13), channel_id=1, source_target_pairs={{0,8},{4,12},{8,0},{12,4},{16,24},{20,28},{24,16},{28,20},{1,9},{5... | collective-permute-start | bytes 98312 | tf_op jit(solution)/shard_map/ppermute | solution.py:54
  16.0 8.3 %collective-permute-start.2 = (bf16[2,1,32,2,128]{4,2,3,1,0:T(8,128)(2,1)S(1)}, bf16[2,1,32,2,128]{4,2,3,1,0:T(8,128)(2,1)S(1)}, u32[]{:S(2)}, u32[]{:S(2)}) collective-permute-start(bf16[2,1,32,2,128]{4,2,3,1,0:T(8,128)(2,1)S(1)} %get-tuple-element.12), channel_id=1, source_target_pairs={{0,12},{4,8},{8,4},{12,0},{16,28},{20,24},{24,20},{28,16},{1,13},{... | collective-permute-start | bytes 98312 | tf_op jit(solution)/shard_map/ppermute | solution.py:54
  16.0 8.4 %collective-permute-start.3 = (bf16[2,1,32,2,128]{4,2,3,1,0:T(8,128)(2,1)S(1)}, bf16[2,1,32,2,128]{4,2,3,1,0:T(8,128)(2,1)S(1)}, u32[]{:S(2)}, u32[]{:S(2)}) collective-permute-start(bf16[2,1,32,2,128]{4,2,3,1,0:T(8,128)(2,1)S(1)} %get-tuple-element.11), channel_id=1, source_target_pairs={{0,16},{4,20},{8,24},{12,28},{16,0},{20,4},{24,8},{28,12},{1,17},{... | collective-permute-start | bytes 98312 | tf_op jit(solution)/shard_map/ppermute | solution.py:54
  19.0 5.7 %collective-permute-start.4 = (bf16[2,1,32,2,128]{4,2,3,1,0:T(8,128)(2,1)S(1)}, bf16[2,1,32,2,128]{4,2,3,1,0:T(8,128)(2,1)S(1)}, u32[]{:S(2)}, u32[]{:S(2)}) collective-permute-start(bf16[2,1,32,2,128]{4,2,3,1,0:T(8,128)(2,1)S(1)} %get-tuple-element.10), channel_id=1, source_target_pairs={{0,20},{4,16},{8,28},{12,24},{16,4},{20,0},{24,12},{28,8},{1,21},{... | collective-permute-start | bytes 98312 | tf_op jit(solution)/shard_map/ppermute | solution.py:54
  20.6 5.8 %collective-permute-start.5 = (bf16[2,1,32,2,128]{4,2,3,1,0:T(8,128)(2,1)S(1)}, bf16[2,1,32,2,128]{4,2,3,1,0:T(8,128)(2,1)S(1)}, u32[]{:S(2)}, u32[]{:S(2)}) collective-permute-start(bf16[2,1,32,2,128]{4,2,3,1,0:T(8,128)(2,1)S(1)} %get-tuple-element.9), channel_id=1, source_target_pairs={{0,24},{4,28},{8,16},{12,20},{16,8},{20,12},{24,0},{28,4},{1,25},{... | collective-permute-start | bytes 98312 | tf_op jit(solution)/shard_map/ppermute | solution.py:54
  24.3 6.7 %collective-permute-start.6 = (bf16[2,1,32,2,128]{4,2,3,1,0:T(8,128)(2,1)S(1)}, bf16[2,1,32,2,128]{4,2,3,1,0:T(8,128)(2,1)S(1)}, u32[]{:S(2)}, u32[]{:S(2)}) collective-permute-start(bf16[2,1,32,2,128]{4,2,3,1,0:T(8,128)(2,1)S(1)} %get-tuple-element.8), channel_id=1, source_target_pairs={{0,28},{4,24},{8,20},{12,16},{16,12},{20,8},{24,4},{28,0},{1,29},{... | collective-permute-start | bytes 98312 | tf_op jit(solution)/shard_map/ppermute | solution.py:54
  31.0 12.3 %copy-start = (s32[2]{0:T(128)S(1)}, s32[2]{0:T(128)}, u32[]{:S(2)}) copy-start(s32[2]{0:T(128)} %param.9) | copy-start | bytes 28
  31.0 13.8 %copy-start.28 = (bf16[128,16,128]{2,1,0:T(8,128)(2,1)S(1)}, bf16[128,16,128]{2,1,0:T(8,128)(2,1)}, u32[]{:S(2)}) copy-start(bf16[128,16,128]{2,1,0:T(8,128)(2,1)} %param.5) | copy-start | bytes 1572868
  31.8 10.9 %collective-permute-start.7 = (bf16[2,16,32,2,128]{4,2,3,0,1:T(8,128)(2,1)S(1)}, bf16[2,16,32,2,128]{4,2,3,0,1:T(8,128)(2,1)S(1)}, u32[]{:S(2)}, u32[]{:S(2)}) collective-permute-start(bf16[2,16,32,2,128]{4,2,3,0,1:T(8,128)(2,1)S(1)} %select_bitcast_fusion), channel_id=1, source_target_pairs={{0,4},{4,0},{8,12},{12,8},{16,20},{20,16},{24,28},{28,24},{1,5},{5... | collective-permute-start | bytes 1572872 | tf_op jit(solution)/shard_map/ppermute | solution.py:13
  43.1 21.2 %collective-permute-start.8 = (bf16[2,16,64,2,128]{4,2,3,0,1:T(8,128)(2,1)S(1)}, bf16[2,16,64,2,128]{4,2,3,0,1:T(8,128)(2,1)S(1)}, u32[]{:S(2)}, u32[]{:S(2)}) collective-permute-start(bf16[2,16,64,2,128]{4,2,3,0,1:T(8,128)(2,1)S(1)} %maximum_select_fusion.1), channel_id=1, source_target_pairs={{0,8},{4,12},{8,0},{12,4},{16,24},{20,28},{24,16},{28,20},{1,9},{5... | collective-permute-start | bytes 3145736 | tf_op jit(solution)/shard_map/ppermute | solution.py:13
  65.4 15.4 %copy-start.24 = (bf16[2,16,128,2,128]{4,2,1,3,0:T(8,128)(2,1)}, bf16[2,16,128,2,128]{4,2,1,3,0:T(8,128)(2,1)S(1)}, u32[]{:S(2)}) copy-start(bf16[2,16,128,2,128]{4,2,1,3,0:T(8,128)(2,1)S(1)} %copy.12) | copy-start | bytes 6291460
  69.0 15.0 %copy-start.1 = (f32[128,2048]{0,1:T(8,128)}, f32[128,2048]{0,1:T(8,128)S(1)}, u32[]{:S(2)}) copy-start(f32[128,2048]{0,1:T(8,128)S(1)} %get-tuple-element.47) | copy-start | bytes 3145732
  70.0 14.8 %copy-start.3 = (f32[128,2048]{0,1:T(8,128)}, f32[128,2048]{0,1:T(8,128)S(1)}, u32[]{:S(2)}) copy-start(f32[128,2048]{0,1:T(8,128)S(1)} %get-tuple-element.45) | copy-start | bytes 3145732
  70.9 14.5 %copy-start.5 = (f32[128,2048]{0,1:T(8,128)}, f32[128,2048]{0,1:T(8,128)S(1)}, u32[]{:S(2)}) copy-start(f32[128,2048]{0,1:T(8,128)S(1)} %get-tuple-element.43) | copy-start | bytes 3145732
  71.8 14.3 %copy-start.7 = (f32[128,2048]{0,1:T(8,128)}, f32[128,2048]{0,1:T(8,128)S(1)}, u32[]{:S(2)}) copy-start(f32[128,2048]{0,1:T(8,128)S(1)} %get-tuple-element.41) | copy-start | bytes 3145732
  72.7 14.0 %copy-start.9 = (f32[128,2048]{0,1:T(8,128)}, f32[128,2048]{0,1:T(8,128)S(1)}, u32[]{:S(2)}) copy-start(f32[128,2048]{0,1:T(8,128)S(1)} %get-tuple-element.39) | copy-start | bytes 3145732
  73.6 14.0 %copy-start.11 = (f32[128,2048]{0,1:T(8,128)}, f32[128,2048]{0,1:T(8,128)S(1)}, u32[]{:S(2)}) copy-start(f32[128,2048]{0,1:T(8,128)S(1)} %get-tuple-element.37) | copy-start | bytes 3145732
  74.7 13.5 %copy-start.13 = (f32[128,2048]{0,1:T(8,128)}, f32[128,2048]{0,1:T(8,128)S(1)}, u32[]{:S(2)}) copy-start(f32[128,2048]{0,1:T(8,128)S(1)} %get-tuple-element.35) | copy-start | bytes 3145732
  75.6 13.3 %copy-start.15 = (f32[128,2048]{0,1:T(8,128)}, f32[128,2048]{0,1:T(8,128)S(1)}, u32[]{:S(2)}) copy-start(f32[128,2048]{0,1:T(8,128)S(1)} %get-tuple-element.33) | copy-start | bytes 3145732
  76.5 13.0 %copy-start.17 = (f32[128,2048]{0,1:T(8,128)}, f32[128,2048]{0,1:T(8,128)S(1)}, u32[]{:S(2)}) copy-start(f32[128,2048]{0,1:T(8,128)S(1)} %get-tuple-element.31) | copy-start | bytes 3145732
  77.4 12.8 %copy-start.19 = (f32[128,2048]{0,1:T(8,128)}, f32[128,2048]{0,1:T(8,128)S(1)}, u32[]{:S(2)}) copy-start(f32[128,2048]{0,1:T(8,128)S(1)} %get-tuple-element.29) | copy-start | bytes 3145732
  78.3 12.5 %copy-start.21 = (f32[128,2048]{0,1:T(8,128)}, f32[128,2048]{0,1:T(8,128)S(1)}, u32[]{:S(2)}) copy-start(f32[128,2048]{0,1:T(8,128)S(1)} %get-tuple-element.27) | copy-start | bytes 3145732
  79.3 12.3 %copy-start.23 = (f32[128,2048]{0,1:T(8,128)}, f32[128,2048]{0,1:T(8,128)S(1)}, u32[]{:S(2)}) copy-start(f32[128,2048]{0,1:T(8,128)S(1)} %get-tuple-element.25) | copy-start | bytes 3145732
  93.9 2.5 %copy-start.22 = (f32[128,2048]{0,1:T(8,128)S(1)}, f32[128,2048]{0,1:T(8,128)}, u32[]{:S(2)}) copy-start(f32[128,2048]{0,1:T(8,128)} %copy-done.21) | copy-start | bytes 3145732
  94.0 2.5 %copy-start.25 = (bf16[2,16,128,2,128]{4,2,1,3,0:T(8,128)(2,1)S(1)}, bf16[2,16,128,2,128]{4,2,1,3,0:T(8,128)(2,1)}, u32[]{:S(2)}) copy-start(bf16[2,16,128,2,128]{4,2,1,3,0:T(8,128)(2,1)} %copy-done.24) | copy-start | bytes 6291460
  97.7 1.2 copy-start.18
  102.6 1.2 copy-start.10
  103.8 1.2 copy-start.8
  106.3 1.2 copy-start.4
  (7 other events, 8.0 us)
Sparse Core Ops, SparseCore 0:
  94.1 58.7 reduce-scatter.1
